TPU v7x, 32 devices: a whole 2x2x4 slice. The times are simulated.
32 devices in a mesh: groups: 2 (over y), seq: 16 (over z, x, core).
Axes of the slice: x: 2, y: 2, z: 4, core: 2. Of those that a mesh axis runs over, the one named last changes fastest.
Arguments:
- queries: bfloat16 [8192, 2048], P(('groups', 'seq')), parts along dimension 0, may hold values from -6 to 6
- keys: bfloat16 [8192, 1024], P(('groups', 'seq')), parts along dimension 0, may hold values from -6 to 6
- values: bfloat16 [8192, 1024], P(('groups', 'seq')), parts along dimension 0, may hold values from -6 to 6
- out_grad: bfloat16 [8192, 2048], P(('groups', 'seq')), parts along dimension 0, may hold values from -6 to 6
Outputs:
- attended: bfloat16 [8192, 2048], P(('groups', 'seq')), parts along dimension 0
- query_grad: bfloat16 [8192, 2048], P(('groups', 'seq')), parts along dimension 0
- key_grad: bfloat16 [8192, 1024], P(('groups', 'seq')), parts along dimension 0
- value_grad: bfloat16 [8192, 1024], P(('groups', 'seq')), parts along dimension 0
There are 2 independent parts, one for each index of `groups`. A program takes and returns all parts, laid end to end along the dimension named above; each array names one. Nothing has to cross between parts.
All inputs are finite; a program needn't handle non-finite values.
Results may differ from a plain program's by a relative error of at most 0.013.
Values may be sent and summed in bfloat16 or wider, within the bound.
A program may use at most 64 MiB of HBM per device.

v0:
```python
import functools

import jax
import jax.numpy as jnp
from jax import lax
from jax.experimental import pallas as pl
from jax.experimental.pallas import tpu as pltpu
from jax.sharding import PartitionSpec as P

HQ = 16
HK = 8
HD = 128
WINDOW = 1024
REACH = 4
LAG = 4

query_scale = 168.0 ** (-0.5)


def product(left, right, left_dim, right_dim):
    return lax.dot_general(
        left, right, (((left_dim,), (right_dim,)), ((), ())), preferred_element_type=jnp.float32
    )


def kernel(
    quads,
    q_hbm,
    g_hbm,
    k_hbm,
    v_hbm,
    att_ref,
    dq_ref,
    dk_ref,
    dv_ref,
    kv,
    gacc,
    gm_out,
    gm_in,
    gx_out,
    gx_in,
    gz_out,
    gz_in,
    part,
    q_ref,
    g_ref,
    own_sem,
    q_sem,
    z_send,
    z_recv,
    x_send,
    x_recv,
    m_send,
    m_recv,
    gz_send,
    gz_recv,
    gx_send,
    gx_recv,
    gm_send,
    gm_recv,
):
    rows = q_hbm.shape[0]
    me = lax.axis_index("seq")
    quad = me // 4
    x = (me // 2) % 2
    core = me % 2
    other = me + 2 - 4 * x
    mate = me + 1 - 2 * core
    has_before = quad > 0
    has_after = quad < quads - 1
    after = jnp.where(has_after, me + 4, me)
    before = jnp.where(has_before, me - 4, me)

    def remote(src, dst, send, recv, target):
        return pltpu.make_async_remote_copy(
            src_ref=src,
            dst_ref=dst,
            send_sem=send,
            recv_sem=recv,
            device_id={"seq": target},
            device_id_type=pl.DeviceIdType.MESH,
        )

    def own_copy(h, which):
        source = (k_hbm, v_hbm)[which]
        return pltpu.make_async_copy(
            source.at[:, pl.ds(pl.multiple_of(h * HD, HD), HD)],
            kv.at[0, h, which],
            own_sem.at[which, h],
        )

    def to_after(h):
        return remote(kv.at[0, h], kv.at[4, h], z_send.at[h], z_recv.at[h], after)

    def to_other(h):
        return remote(kv.at[4 * x, h], kv.at[2, h], x_send.at[h], x_recv.at[h], other)

    def to_mate_a(h):
        return remote(
            kv.at[2, h], kv.at[3 - 2 * core, h], m_send.at[0, h], m_recv.at[0, h], mate
        )

    def to_mate_b(h):
        return remote(
            kv.at[4 * core, h], kv.at[1 + 2 * core, h], m_send.at[1, h], m_recv.at[1, h], mate
        )

    def grad_mate(h, which):
        return remote(
            gm_out.at[which, h],
            gm_in.at[which, h],
            gm_send.at[which, h],
            gm_recv.at[which, h],
            mate,
        )

    def grad_other(h):
        return remote(gx_out.at[h], gx_in.at[h], gx_send.at[h], gx_recv.at[h], other)

    def grad_before(h):
        return remote(gz_out.at[h], gz_in.at[h], gz_send.at[h], gz_recv.at[h], before)

    for h in range(HK):
        own_copy(h, 0).start()
        own_copy(h, 1).start()
    query_copy = pltpu.make_async_copy(q_hbm, q_ref, q_sem.at[0])
    grad_copy = pltpu.make_async_copy(g_hbm, g_ref, q_sem.at[1])
    query_copy.start()
    grad_copy.start()

    barrier = pltpu.get_barrier_semaphore()
    for target in (other, mate):
        pl.semaphore_signal(
            barrier, inc=1, device_id={"seq": target}, device_id_type=pl.DeviceIdType.MESH
        )

    @pl.when(has_before)
    def _():
        pl.semaphore_signal(
            barrier, inc=1, device_id={"seq": before}, device_id_type=pl.DeviceIdType.MESH
        )

    @pl.when(has_after)
    def _():
        pl.semaphore_signal(
            barrier, inc=1, device_id={"seq": after}, device_id_type=pl.DeviceIdType.MESH
        )

    @pl.when(jnp.logical_not(has_before))
    def _():
        kv[4] = jnp.zeros(kv.shape[1:], kv.dtype)

    pl.semaphore_wait(
        barrier, 2 + jnp.where(has_before, 1, 0) + jnp.where(has_after, 1, 0)
    )

    def start_after(h, carry):
        own_copy(h, 0).wait()
        own_copy(h, 1).wait()

        @pl.when(has_after)
        def _():
            to_after(h).start()

        @pl.when(x == 0)
        def _():
            to_other(h).start()

        return carry

    lax.fori_loop(0, HK, start_after, 0)

    def stage_other(h):
        @pl.when(has_before)
        def _():
            to_after(h).wait_recv()

        @pl.when(x == 1)
        def _():
            to_other(h).start()

    def stage_mate(h):
        to_other(h).wait_recv()
        to_mate_a(h).start()
        to_mate_b(h).start()

    key_ids = lax.broadcasted_iota(jnp.int32, (rows, rows), 0)
    query_ids = lax.broadcasted_iota(jnp.int32, (rows, rows), 1)

    def attend(h, j, last):
        extent = (REACH + 1) * rows
        key_all = kv[:, h, 0].reshape(extent, HD)
        value_all = kv[:, h, 1].reshape(extent, HD)
        columns = pl.ds(pl.multiple_of(h * (HQ // HK * HD) + j * HD, HD), HD)
        query = q_ref[:, columns]
        grad = g_ref[:, columns]
        scores = product(key_all, query, 1, 1) * query_scale
        parts = [scores[d * rows : (d + 1) * rows] for d in range(REACH + 1)]
        parts[0] = jnp.where(key_ids <= query_ids, parts[0], jnp.float32(-1e30))
        parts[REACH] = jnp.where(key_ids > query_ids, parts[REACH], jnp.float32(-1e30))
        outside = [jnp.where(me >= d, jnp.float32(0), jnp.float32(1e30)) for d in range(REACH + 1)]
        peak = jnp.max(parts[0], axis=0, keepdims=True)
        for d in range(1, REACH + 1):
            peak = jnp.maximum(peak, jnp.max(parts[d], axis=0, keepdims=True) - outside[d])
        expo = jnp.concatenate(
            [jnp.exp(parts[d] - (peak + outside[d])) for d in range(REACH + 1)], axis=0
        )
        prob = expo * (1.0 / jnp.sum(expo, axis=0, keepdims=True))
        prob_b = prob.astype(jnp.bfloat16)
        attended = product(value_all, prob_b, 0, 0)
        att_ref[:, columns] = attended.T.astype(jnp.bfloat16)
        delta = jnp.sum(attended * grad.astype(jnp.float32).T, axis=0, keepdims=True)
        dprob = product(value_all, grad, 1, 1)
        dscore = (query_scale * prob * (dprob - delta)).astype(jnp.bfloat16)
        query_grad = product(key_all, dscore, 0, 0)
        dq_ref[:, columns] = query_grad.T.astype(jnp.bfloat16)
        for which, total in enumerate((product(dscore, query, 1, 0), product(prob_b, grad, 1, 0))):
            if not last:
                part[which] = total
                continue
            total = total + part[which]
            pieces = [total[d * rows : (d + 1) * rows] for d in range(REACH + 1)]
            gm_out[core, h, which] = pieces[1].astype(jnp.bfloat16)
            gm_out[1 - core, h, which] = pieces[3].astype(jnp.bfloat16)
            for place in range(3):
                gacc[place, h, which] = pieces[2 * place]

    def stage_grad_other(h):
        grad_mate(h, 0).wait_recv()
        grad_mate(h, 1).wait_recv()
        gacc[1, h] += gm_in[0, h].astype(jnp.float32)
        gacc[2 * core, h] += gm_in[1, h].astype(jnp.float32)
        gx_out[h] = gacc[1, h].astype(jnp.bfloat16)
        grad_other(h).start()

        @pl.when(has_before & (x == 0))
        def _():
            gz_out[h] = gacc[2, h].astype(jnp.bfloat16)
            grad_before(h).start()

    def stage_grad_before(h):
        grad_other(h).wait_recv()
        gacc[2 * x, h] += gx_in[h].astype(jnp.float32)

        @pl.when(has_before & (x == 1))
        def _():
            gz_out[h] = gacc[2, h].astype(jnp.bfloat16)
            grad_before(h).start()

    def stage_final(h):
        @pl.when(has_after)
        def _():
            grad_before(h).wait_recv()
            gacc[0, h] += gz_in[h].astype(jnp.float32)

        columns = pl.ds(pl.multiple_of(h * HD, HD), HD)
        dk_ref[:, columns] = gacc[0, h, 0].astype(jnp.bfloat16)
        dv_ref[:, columns] = gacc[0, h, 1].astype(jnp.bfloat16)

    stage_other(0)
    stage_other(1)
    stage_mate(0)
    query_copy.wait()
    grad_copy.wait()
    stage_other(2)

    def step(i, carry):
        @pl.when((i >= 1) & (2 * i + 2 < HK))
        def _():
            stage_other(2 * i + 2)

        remote(
            kv.at[2, i], kv.at[1 + 2 * core, i], m_send.at[0, i], m_recv.at[0, i], mate
        ).wait_recv()
        remote(
            kv.at[0, i], kv.at[3 - 2 * core, i], m_send.at[1, i], m_recv.at[1, i], mate
        ).wait_recv()
        attend(i, 0, False)

        @pl.when(2 * i + 3 < HK)
        def _():
            stage_other(2 * i + 3)

        @pl.when(i + 1 < HK)
        def _():
            stage_mate(i + 1)

        @pl.when(i >= 1)
        def _():
            stage_grad_other(i - 1)

        @pl.when(i >= LAG)
        def _():
            stage_grad_before(i - LAG)

        attend(i, 1, True)
        grad_mate(i, 0).start()
        grad_mate(i, 1).start()
        return carry

    lax.fori_loop(0, HK, step, 0)
    stage_grad_other(HK - 1)

    def drain(n, carry):
        stage_grad_before(n + HK - LAG)

        @pl.when(n < HK - LAG)
        def _():
            stage_final(n)

        return carry

    lax.fori_loop(0, LAG, drain, 0)

    def last_final(h, carry):
        stage_final(h)
        return carry

    lax.fori_loop(min(LAG, HK - LAG), HK, last_final, 0)

    def finish(h, carry):
        @pl.when(has_after)
        def _():
            to_after(h).wait_send()

        to_other(h).wait_send()
        to_mate_a(h).wait_send()
        to_mate_b(h).wait_send()
        grad_mate(h, 0).wait_send()
        grad_mate(h, 1).wait_send()
        grad_other(h).wait_send()

        @pl.when(has_before)
        def _():
            grad_before(h).wait_send()

        return carry

    lax.fori_loop(0, HK, finish, 0)


def per_device(quads, queries, keys, values, out_grad):
    rows = queries.shape[0]
    pair = (2, rows, HD)
    one = pltpu.SemaphoreType.DMA((HK,))
    two = pltpu.SemaphoreType.DMA((2, HK))
    vmem = pl.BlockSpec(memory_space=pltpu.VMEM)
    hbm = pl.BlockSpec(memory_space=pltpu.HBM)
    return pl.pallas_call(
        functools.partial(kernel, quads),
        out_shape=(
            jax.ShapeDtypeStruct(queries.shape, jnp.bfloat16),
            jax.ShapeDtypeStruct(queries.shape, jnp.bfloat16),
            jax.ShapeDtypeStruct(keys.shape, jnp.bfloat16),
            jax.ShapeDtypeStruct(keys.shape, jnp.bfloat16),
        ),
        in_specs=[hbm, hbm, hbm, hbm],
        out_specs=(vmem, vmem, vmem, vmem),
        scratch_shapes=[
            pltpu.VMEM((REACH + 1, HK) + pair, jnp.bfloat16),
            pltpu.VMEM((3, HK) + pair, jnp.float32),
            pltpu.VMEM((2, HK) + pair, jnp.bfloat16),
            pltpu.VMEM((2, HK) + pair, jnp.bfloat16),
            pltpu.VMEM((HK,) + pair, jnp.bfloat16),
            pltpu.VMEM((HK,) + pair, jnp.bfloat16),
            pltpu.VMEM((HK,) + pair, jnp.bfloat16),
            pltpu.VMEM((HK,) + pair, jnp.bfloat16),
            pltpu.VMEM((2, (REACH + 1) * rows, HD), jnp.float32),
            pltpu.VMEM(queries.shape, jnp.bfloat16),
            pltpu.VMEM(queries.shape, jnp.bfloat16),
            two,
            pltpu.SemaphoreType.DMA((2,)),
            one,
            one,
            one,
            one,
            two,
            two,
            one,
            one,
            one,
            one,
            two,
            two,
        ],
        compiler_params=pltpu.CompilerParams(
            collective_id=0, has_side_effects=True, vmem_limit_bytes=42000 * 1024
        ),
    )(
        *(
            pltpu.with_memory_space_constraint(array, pltpu.HBM)
            for array in (queries, out_grad, keys, values)
        )
    )


def solution(mesh):
    spec = P(("groups", "seq"), None)
    return jax.shard_map(
        functools.partial(per_device, mesh.shape["seq"] // 4),
        mesh=mesh,
        in_specs=(spec, spec, spec, spec),
        out_specs=(spec, spec, spec, spec),
        check_vma=False,
    )
```

profile of v0, /device:TPU:19, one launch (start us, length us, event | category | flops | bytes accessed | tf_op | source)
XLA Modules:
  0.0 69.1 jit_solution(9827013762311216611)
XLA Ops:
  0.6 64.9 %shard_map.75 = (bf16[256,2048]{1,0:T(8,128)(2,1)S(1)}, bf16[256,2048]{1,0:T(8,128)(2,1)S(1)}, bf16[256,1024]{1,0:T(8,128)(2,1)S(1)}, bf16[256,1024]{1,0:T(8,128)(2,1)S(1)}) custom-call(bf16[256,2048]{1,0:T(8,128)(2,1)} %q_hbm.1, bf16[256,2048]{1,0:T(8,128)(2,1)} %g_hbm.1, bf16[256,1024]{1,0:T(8,128)(2,1)} %k_hbm.1, bf16[256,1024]{1,0:T(8,128)(2,1)} %v_hbm.1), custom_call_target="tpu_custom_call" | custom-call | tf_op jit(solution)/shard_map/pallas_call | solution.py:349
  65.6 1.0 %copy.12 = bf16[256,2048]{1,0:T(8,128)(2,1)} copy(bf16[256,2048]{1,0:T(8,128)(2,1)S(1)} %get-tuple-element.8) | data formatting | bytes 2097152
  66.5 1.0 %copy.13 = bf16[256,2048]{1,0:T(8,128)(2,1)} copy(bf16[256,2048]{1,0:T(8,128)(2,1)S(1)} %get-tuple-element.9) | data formatting | bytes 2097152
  67.5 0.8 %copy.14 = bf16[256,1024]{1,0:T(8,128)(2,1)} copy(bf16[256,1024]{1,0:T(8,128)(2,1)S(1)} %get-tuple-element.10) | data formatting | bytes 1048576
  68.3 0.8 %copy.15 = bf16[256,1024]{1,0:T(8,128)(2,1)} copy(bf16[256,1024]{1,0:T(8,128)(2,1)S(1)} %get-tuple-element.11) | data formatting | bytes 1048576
where the time goes:
time: 69.2 us; the launch traced here: 69.1 us
  Pallas kernels  64.9 us (94%)
  local copies, waits for them, and re-layouts  3.53 us (5%)
    pallas_call x1, Pallas kernels, per_device(): pl.pallas_call(functools.partial(kernel, quads), out_shape=(jax.ShapeDtyp...  64.9 us
    unnamed x4, local copies, waits for them, and re-layouts  3.53 us

commit v1 on v0

--- a/solution.py
+++ b/solution.py
@@ -12,9 +12,10 @@
 HD = 128
 WINDOW = 1024
 REACH = 4
-LAG = 4
+LAG = 3
 
 query_scale = 168.0 ** (-0.5)
+exponent_scale = query_scale * 1.4426950408889634
 
 
 def product(left, right, left_dim, right_dim):
@@ -194,7 +195,7 @@
         columns = pl.ds(pl.multiple_of(h * (HQ // HK * HD) + j * HD, HD), HD)
         query = q_ref[:, columns]
         grad = g_ref[:, columns]
-        scores = product(key_all, query, 1, 1) * query_scale
+        scores = product(key_all, query, 1, 1)
         parts = [scores[d * rows : (d + 1) * rows] for d in range(REACH + 1)]
         parts[0] = jnp.where(key_ids <= query_ids, parts[0], jnp.float32(-1e30))
         parts[REACH] = jnp.where(key_ids > query_ids, parts[REACH], jnp.float32(-1e30))
@@ -203,7 +204,11 @@
         for d in range(1, REACH + 1):
             peak = jnp.maximum(peak, jnp.max(parts[d], axis=0, keepdims=True) - outside[d])
         expo = jnp.concatenate(
-            [jnp.exp(parts[d] - (peak + outside[d])) for d in range(REACH + 1)], axis=0
+            [
+                jnp.exp2((parts[d] - (peak + outside[d])) * exponent_scale)
+                for d in range(REACH + 1)
+            ],
+            axis=0,
         )
         prob = expo * (1.0 / jnp.sum(expo, axis=0, keepdims=True))
         prob_b = prob.astype(jnp.bfloat16)

time: 69.2 us -> 68.7 us (level)
  Pallas kernels: 64.9 us -> 63.8 us
    pallas_call x1, Pallas kernels: 64.9 us -> 63.8 us  [per_device(): pl.pallas_call(functools.partial(kernel, quads), out_shape=(jax.ShapeDtyp...]
where the time goes in v1:
time: 68.7 us; the launch traced here: 68 us
  Pallas kernels  63.8 us (93%)
  local copies, waits for them, and re-layouts  3.53 us (5%)
    pallas_call x1, Pallas kernels, per_device(): pl.pallas_call(functools.partial(kernel, quads), out_shape=(jax.ShapeDtyp...  63.8 us
    unnamed x4, local copies, waits for them, and re-layouts  3.53 us

profile of v1, /device:TPU:19, one launch (start us, length us, event | category | flops | bytes accessed | tf_op | source)
XLA Modules:
  0.0 68.0 jit_solution(103294502992162811)
XLA Ops:
  0.6 63.8 %shard_map.75 = (bf16[256,2048]{1,0:T(8,128)(2,1)S(1)}, bf16[256,2048]{1,0:T(8,128)(2,1)S(1)}, bf16[256,1024]{1,0:T(8,128)(2,1)S(1)}, bf16[256,1024]{1,0:T(8,128)(2,1)S(1)}) custom-call(bf16[256,2048]{1,0:T(8,128)(2,1)} %q_hbm.1, bf16[256,2048]{1,0:T(8,128)(2,1)} %g_hbm.1, bf16[256,1024]{1,0:T(8,128)(2,1)} %k_hbm.1, bf16[256,1024]{1,0:T(8,128)(2,1)} %v_hbm.1), custom_call_target="tpu_custom_call" | custom-call | tf_op jit(solution)/shard_map/pallas_call | solution.py:354
  64.4 1.0 %copy.12 = bf16[256,2048]{1,0:T(8,128)(2,1)} copy(bf16[256,2048]{1,0:T(8,128)(2,1)S(1)} %get-tuple-element.8) | data formatting | bytes 2097152
  65.4 1.0 %copy.13 = bf16[256,2048]{1,0:T(8,128)(2,1)} copy(bf16[256,2048]{1,0:T(8,128)(2,1)S(1)} %get-tuple-element.9) | data formatting | bytes 2097152
  66.4 0.8 %copy.14 = bf16[256,1024]{1,0:T(8,128)(2,1)} copy(bf16[256,1024]{1,0:T(8,128)(2,1)S(1)} %get-tuple-element.10) | data formatting | bytes 1048576
  67.2 0.8 %copy.15 = bf16[256,1024]{1,0:T(8,128)(2,1)} copy(bf16[256,1024]{1,0:T(8,128)(2,1)S(1)} %get-tuple-element.11) | data formatting | bytes 1048576
